TPU v7x, 256 devices: a whole 4x4x8 slice. The times are simulated.
256 devices in a mesh: seq: 16 (over y_lo, z), chan: 16 (over y_hi, x, core).
Axes of the slice: x: 4, y: 4 (y_hi: 2, y_lo: 2; y = y_hi * 2 + y_lo), z: 8, core: 2. Of those that a mesh axis runs over, the one named last changes fastest.
Arguments:
- tokens: bfloat16 [8192, 8192], P('seq', 'chan'), may hold values from -6 to 6
- norm_gain: float32 [8192], replicated, may hold values from 0.1 to 1.9
- w_in: bfloat16 [8192, 3, 4096], P('seq', None, 'chan'), may hold values from -0.0625 to 0.0625
- short_taps: float32 [3, 3, 4096], P(None, None, 'chan'), may hold values from -3.6 to 3.6
- medium_taps: float32 [128, 256], P(None, 'chan'), may hold values from -0.75 to 0.75
- skip_gain: float32 [4096], P('chan'), may hold values from 0.5 to 1.5
- w_out: bfloat16 [4096, 8192], P('chan'), may hold values from -0.09375 to 0.09375
Outputs:
- block_out: bfloat16 [8192, 8192], P('seq', 'chan')
All inputs are finite; a program needn't handle non-finite values.
Results may differ from a plain program's by a relative error of at most 0.019.
Values may be sent and summed in bfloat16 or wider, within the bound.
A program may use at most 128 MiB of HBM per device.

v0:
```python
import jax
import jax.numpy as jnp
from jax import lax
from jax.sharding import PartitionSpec as P

TAPS = 128
GROUP = 16
EPSILON = 1e-06


def passed_along(value, axis, steps):
    count = lax.axis_size(axis)
    first, last = (max(0, -steps), min(count, count - steps))
    return lax.ppermute(value, axis, [(source, source + steps) for source in range(first, last)])


def short_filter(extended, taps):
    return taps[0] * extended[2:] + taps[1] * extended[1:-1] + taps[2] * extended[:-2]


def per_device(tokens, norm_gain, w_in, short_taps, medium_taps, skip_gain, w_out):
    row_count = tokens.shape[0]
    channels = w_in.shape[2]
    gathered = lax.all_gather(tokens, "chan", axis=1, tiled=True)
    widened = gathered.astype(jnp.float32)
    mean_square = jnp.mean(widened * widened, axis=1, keepdims=True)
    normed = (widened * lax.rsqrt(mean_square + EPSILON) * norm_gain).astype(jnp.bfloat16)
    section = lax.all_gather(w_in, "seq", axis=0, tiled=True)
    flat_section = section.reshape(section.shape[0], 3 * channels)
    summed = jnp.dot(normed, flat_section, preferred_element_type=jnp.float32)
    projected = summed.astype(jnp.bfloat16).reshape(row_count, 3, channels)
    edge_rows = passed_along(projected[row_count - 2 :], "seq", 1)
    extended = lax.optimization_barrier(jnp.concatenate([edge_rows, projected], 0)).astype(
        jnp.float32
    )
    filtered = short_filter(extended, short_taps)
    queries = filtered[:, 0]
    product = (filtered[:, 1] * filtered[:, 2]).astype(jnp.bfloat16)
    product_rows = passed_along(product[row_count - (TAPS - 1) :], "seq", 1)
    reached = jnp.concatenate([product_rows, product], 0)
    floats = lax.optimization_barrier(reached).astype(jnp.float32)
    padded = jnp.concatenate([jnp.zeros((1, channels), jnp.float32), floats], 0)
    block_count = row_count // TAPS
    blocks = padded.reshape(block_count + 1, TAPS, channels)
    windows = jnp.concatenate([blocks[:-1], blocks[1:]], 1)
    cube_shape = (TAPS, TAPS, 2 * TAPS)
    lagged = (
        lax.broadcasted_iota(jnp.int32, cube_shape, 1)
        + TAPS
        - lax.broadcasted_iota(jnp.int32, cube_shape, 2)
    )
    onehot = (lagged == lax.broadcasted_iota(jnp.int32, cube_shape, 0)).astype(jnp.float32)
    toeplitz = jnp.einsum("jg,jis->gis", medium_taps, onehot, precision=lax.Precision.HIGHEST)
    filters = medium_taps.shape[1]
    grouped = windows.reshape(block_count, 2 * TAPS, filters, GROUP)
    convolved = jnp.einsum("gis,bsgc->bigc", toeplitz, grouped, precision=lax.Precision.HIGHEST)
    mixing = skip_gain * floats[TAPS - 1 :] + convolved.reshape(row_count, channels)
    gating = (queries * mixing).astype(jnp.bfloat16)
    partial_out = jnp.dot(gating, w_out, preferred_element_type=jnp.float32)
    rounded_out = lax.optimization_barrier(partial_out.astype(jnp.bfloat16)).astype(jnp.float32)
    projected_out = lax.psum_scatter(
        rounded_out.astype(jnp.bfloat16), "chan", scatter_dimension=1, tiled=True
    ).astype(jnp.float32)
    return (tokens.astype(jnp.float32) + projected_out).astype(jnp.bfloat16)


def solution(mesh):
    in_specs = (
        P("seq", "chan"),
        P(),
        P("seq", None, "chan"),
        P(None, None, "chan"),
        P(None, "chan"),
        P("chan"),
        P("chan", None),
    )
    out_specs = P("seq", "chan")
    return jax.shard_map(
        per_device, mesh=mesh, in_specs=in_specs, out_specs=out_specs, check_vma=False
    )
```

profile of v0, /device:TPU:2, one launch (start us, length us, event | category | flops | bytes accessed | tf_op | source)
XLA Modules:
  0.0 403.7 jit_solution(17343954570505300916)
XLA Ops:
  6.5 0.7 all-gather.3.cloned.1.call-update
  7.3 2.3 copy.10
  9.7 2.6 iota_compare_fusion
  12.3 9.2 %fusion.3 = f32[128,256,16]{1,2,0:T(8,128)} fusion(pred[128,128,256]{2,1,0:T(32,128)(4,1)S(1)} %iota_compare_fusion, f32[128,16]{0,1:T(8,128)S(1)} %copy-done), kind=kOutput, calls=%fused_computation.6 | convolution fusion | flops 805306368 | bytes 6299648 | tf_op jit(solution)/shard_map/jg,jis->gis/dot_general | solution.py:53
  21.5 76.3 %all-gather.3.cloned.1.call-done = bf16[512,8192]{1,0:T(8,128)(2,1)} async-done(((bf16[512,512]{1,0:T(8,128)(2,1)}), bf16[512,8192]{1,0:T(8,128)(2,1)}) %all-gather.3.cloned.1.call-update) | async-done | bytes 8388624 | tf_op jit(solution)/shard_map/all_gather | solution.py:24
  97.8 5.1 %fusion = f32[512]{0:T(512)S(1)} fusion(bf16[512,8192]{1,0:T(8,128)(2,1)} %all-gather.3.cloned.1.call-done), kind=kLoop, calls=%fused_computation.2 | loop fusion | flops 12582400 | bytes 8390656 | tf_op jit(solution)/shard_map/reduce_sum | solution.py:26
  102.9 138.7 %all-gather.5.cloned.1.call-done = bf16[8192,3,256]{0,2,1:T(8,128)(2,1)} async-done(((bf16[512,3,256]{0,2,1:T(8,128)(2,1)}), bf16[8192,3,256]{0,2,1:T(8,128)(2,1)}) %all-gather.5.cloned.1.call-update) | async-done | bytes 12582928 | tf_op jit(solution)/shard_map/all_gather | solution.py:28
  241.6 13.1 %fusion.14 = bf16[512,768]{1,0:T(8,128)(2,1)S(1)} fusion(bf16[8192,768]{0,1:T(8,128)(2,1)} %bitcast.50, bf16[512,8192]{1,0:T(8,128)(2,1)} %all-gather.3.cloned.1.call-done, f32[8192]{0:T(1024)S(1)} %copy-done.5, f32[512]{0:T(512)S(1)} %add_rsqrt_fusion), kind=kOutput, calls=%fused_computation.20 | convolution fusion | flops 6459621376 | bytes 21792768 | tf_op jit(solution)/shard_map/dot_general | solution.py:30
  254.8 1.3 collective-permute-start
  256.1 0.3 copy.11
  256.4 1.0 collective-permute-done
  257.6 0.5 pad_maximum_fusion
  258.2 1.4 fusion.12
  259.8 4.4 %collective-permute-start.1 = (bf16[127,256]{0,1:T(8,128)(2,1)S(1)}, bf16[127,256]{0,1:T(8,128)(2,1)S(1)}, u32[]{:S(2)}, u32[]{:S(2)}) collective-permute-start(bf16[127,256]{0,1:T(8,128)(2,1)S(1)} %slice_bitcast_fusion.1), channel_id=1, source_target_pairs={{0,16},{16,32},{32,48},{48,64},{64,80},{80,96},{96,112},{112,128},... | collective-permute-start | bytes 195080 | tf_op jit(solution)/shard_map/ppermute | solution.py:14
  264.3 1.6 collective-permute-done.1
  266.4 1.0 concatenate.20
  267.4 1.1 copy.15
  268.5 1.0 concatenate.21
  269.4 1.2 copy.16
  270.7 5.2 %fusion.17 = f32[4,128,16,16]{1,3,0,2:T(8,128)S(1)} fusion(f32[128,256,16]{1,2,0:T(8,128)} %fusion.3, f32[4,128,16,16]{1,3,0,2:T(8,128)S(1)} %copy.16, f32[4,128,16,16]{1,3,0,2:T(8,128)S(1)} %copy.15), kind=kOutput, calls=%fused_computation.21 | convolution fusion | flops 402915328 | bytes 3670016 | tf_op jit(solution)/shard_map/gis,bsgc->bigc/dot_general | solution.py:56
  275.8 0.2 copy.17
  276.1 5.9 %convolution_convert_fusion = bf16[512,8192]{1,0:T(8,128)(2,1)} fusion(bf16[256,8192]{1,0:T(8,128)(2,1)S(1)} %copy-done.1, f32[32,8,4,128]{3,2,1,0:T(4,128)S(1)} %bitcast.49, f32[512,3,256]{0,2,1:T(8,128)S(1)} %fusion.12, f32[256]{0:T(256)S(1)} %copy-done.3, f32[639,256]{0,1:T(8,128)S(1)} %convert_element_type.46), kind=kOutput, calls=%fused_computation.8 | convolution fusion | flops 2152202240 | bytes 14156800 | tf_op jit(solution)/shard_map/dot_general | solution.py:59
  282.0 113.2 %reduce-scatter.2.cloned.1.call-done = bf16[512,512]{1,0:T(8,128)(2,1)} async-done(((bf16[512,8192]{1,0:T(8,128)(2,1)}), bf16[512,512]{1,0:T(8,128)(2,1)}) %reduce-scatter.2.cloned.1.call-update) | async-done | bytes 524304 | tf_op jit(solution)/shard_map/reduce_scatter | solution.py:61
  395.2 2.0 add_convert_fusion
  (31 shorter events, 1.3 us)
Async XLA Ops:
  6.5 5.8 %copy-start = (f32[128,16]{0,1:T(8,128)S(1)}, f32[128,16]{0,1:T(8,128)}, u32[]{:S(2)}) copy-start(f32[128,16]{0,1:T(8,128)} %param.11) | copy-start | bytes 24580
  6.5 91.3 %all-gather.3.cloned.1.call-start = ((), (), s32[]{:S(2)}) async-start(), calls=%async_computation.1 | async-start | bytes 8912896 | tf_op jit(solution)/shard_map/all_gather | solution.py:24
  7.3 234.3 %all-gather.5.cloned.1.call-start = ((), (), s32[]{:S(2)}) async-start(), calls=%async_computation.2 | async-start | bytes 13369344 | tf_op jit(solution)/shard_map/all_gather | solution.py:28
  9.6 385.6 %reduce-scatter.2.cloned.1.call-start = ((), (), s32[]{:S(2)}) async-start(), calls=%async_computation.3 | async-start | bytes 8912896 | tf_op jit(solution)/shard_map/reduce_scatter | solution.py:61
  21.5 220.1 %copy-start.5 = (f32[8192]{0:T(1024)S(1)}, f32[8192]{0:T(1024)}, u32[]{:S(2)}) copy-start(f32[8192]{0:T(1024)} %param.8) | copy-start | bytes 98308
  241.6 14.5 %copy-start.4 = (f32[3,3,256]{2,1,0:T(4,128)S(1)}, f32[3,3,256]{2,1,0:T(4,128)}, u32[]{:S(2)}) copy-start(f32[3,3,256]{2,1,0:T(4,128)} %param.10) | copy-start | bytes 27652
  254.8 2.6 collective-permute-start
  259.8 6.1 %collective-permute-start.1 = (bf16[127,256]{0,1:T(8,128)(2,1)S(1)}, bf16[127,256]{0,1:T(8,128)(2,1)S(1)}, u32[]{:S(2)}, u32[]{:S(2)}) collective-permute-start(bf16[127,256]{0,1:T(8,128)(2,1)S(1)} %slice_bitcast_fusion.1), channel_id=1, source_target_pairs={{0,16},{16,32},{32,48},{48,64},{64,80},{80,96},{96,112},{112,128},... | collective-permute-start | bytes 195080 | tf_op jit(solution)/shard_map/ppermute | solution.py:14
  267.4 8.7 %copy-start.3 = (f32[256]{0:T(256)S(1)}, f32[256]{0:T(256)}, u32[]{:S(2)}) copy-start(f32[256]{0:T(256)} %param.12) | copy-start | bytes 3076
  269.4 6.6 %copy-start.1 = (bf16[256,8192]{1,0:T(8,128)(2,1)S(1)}, bf16[256,8192]{1,0:T(8,128)(2,1)}, u32[]{:S(2)}) copy-start(bf16[256,8192]{1,0:T(8,128)(2,1)} %param.13) | copy-start | bytes 12582916
  282.0 113.2 %copy-start.2 = (bf16[512,512]{1,0:T(8,128)(2,1)S(1)}, bf16[512,512]{1,0:T(8,128)(2,1)}, u32[]{:S(2)}) copy-start(bf16[512,512]{1,0:T(8,128)(2,1)} %param.7) | copy-start | bytes 1572868
Sparse Core Ops, SparseCore 0:
  9.9 87.8 all-gather.2
  99.6 141.9 all-gather.4
  282.2 113.0 reduce-scatter.1
where the time goes:
time: 404 us
  waiting for transfers between devices  332 us (82%)
  matrix products  33.4 us (8%)
  between operations  13.3 us (3%)
  other arithmetic  12 us (3%)
  local copies, waits for them, and re-layouts  7.71 us (2%)
  starting transfers between devices  5.78 us (1%)
    all_gather x1, waiting for transfers between devices, per_device(): section = lax.all_gather(w_in, 'seq', axis=0, tiled=True)  139 us
    reduce_scatter x1, waiting for transfers between devices, per_device(): lax.psum_scatter(rounded_out.astype(jnp.bfloat16), 'chan', scatter_dimens...  113 us
    all_gather x1, waiting for transfers between devices, per_device(): gathered = lax.all_gather(tokens, 'chan', axis=1, tiled=True)  76.3 us
    dot_general x1, matrix products, per_device(): summed = jnp.dot(normed, flat_section, preferred_element_type=jnp.float32)  13.1 us
    dot_general x1, matrix products, per_device(): jnp.einsum('jg,jis->gis', medium_taps, onehot, precision=lax.Precision.HI...  9.22 us
  transfers between devices with their start and end apart: 5, of which 5 were waited for; matrix products, arithmetic and copies ran while one was open for 5% of the time, Pallas kernels for 0%

commit v1 on v0

--- a/solution.py
+++ b/solution.py
@@ -21,7 +21,9 @@
 def per_device(tokens, norm_gain, w_in, short_taps, medium_taps, skip_gain, w_out):
     row_count = tokens.shape[0]
     channels = w_in.shape[2]
-    gathered = lax.all_gather(tokens, "chan", axis=1, tiled=True)
+    gathered = jnp.concatenate(
+        lax.all_to_all(jnp.stack([tokens] * lax.axis_size("chan")), "chan", 0, 0), axis=1
+    )
     widened = gathered.astype(jnp.float32)
     mean_square = jnp.mean(widened * widened, axis=1, keepdims=True)
     normed = (widened * lax.rsqrt(mean_square + EPSILON) * norm_gain).astype(jnp.bfloat16)

time: 404 us -> 416 us (1.030)
  waiting for transfers between devices: 332 us -> 322 us
  other arithmetic: 12 us -> 19.8 us
  starting transfers between devices: 5.78 us -> 13.4 us
  local copies, waits for them, and re-layouts: 7.71 us -> 13.1 us
    all_to_all x0 -> x1, waiting for transfers between devices: none -> 208 us  [per_device(): lax.all_to_all(jnp.stack([tokens] * lax.axis_size('chan')), 'chan', 0, 0)]
    all_gather x1, waiting for transfers between devices: 139 us -> 0.01 us  [per_device(): section = lax.all_gather(w_in, 'seq', axis=0, tiled=True)]
    all_gather x1 -> x0, waiting for transfers between devices: 76.3 us -> none  [per_device(): gathered = lax.all_gather(tokens, 'chan', axis=1, tiled=True)]
    convert_element_type x0 -> x1, other arithmetic: none -> 7.75 us  [per_device(): (widened * lax.rsqrt(mean_square + EPSILON) * norm_gain).astype(jnp.bfloa...]
    all_to_all x0 -> x1, starting transfers between devices: none -> 7.61 us  [per_device(): lax.all_to_all(jnp.stack([tokens] * lax.axis_size('chan')), 'chan', 0, 0)]
  transfers between devices with their start and end apart: 5 -> 5, of which waited for: 5 -> 4; matrix products, arithmetic and copies ran while one was open for 5% -> 7% of each run, Pallas kernels for 0% -> 0%
where the time goes in v1:
time: 416 us; the launch traced here: 415 us
  waiting for transfers between devices  322 us (77%)
  matrix products  33.4 us (8%)
  other arithmetic  19.8 us (5%)
  between operations  13.6 us (3%)
  starting transfers between devices  13.4 us (3%)
  local copies, waits for them, and re-layouts  13.1 us (3%)
    all_to_all x1, waiting for transfers between devices, per_device(): lax.all_to_all(jnp.stack([tokens] * lax.axis_size('chan')), 'chan', 0, 0)  208 us
    reduce_scatter x1, waiting for transfers between devices, per_device(): lax.psum_scatter(rounded_out.astype(jnp.bfloat16), 'chan', scatter_dimens...  112 us
    dot_general x1, matrix products, per_device(): summed = jnp.dot(normed, flat_section, preferred_element_type=jnp.float32)  12.9 us
    dot_general x1, matrix products, per_device(): jnp.einsum('jg,jis->gis', medium_taps, onehot, precision=lax.Precision.HI...  9.4 us
  transfers between devices with their start and end apart: 5, of which 4 were waited for; matrix products, arithmetic and copies ran while one was open for 7% of the time, Pallas kernels for 0%

profile of v1, /device:TPU:2, one launch (start us, length us, event | category | flops | bytes accessed | tf_op | source)
XLA Modules:
  0.0 415.3 jit_solution(8571033909812756365)
XLA Ops:
  6.5 2.3 copy.11
  8.9 1.3 copy.10
  10.1 4.1 stack.2
  14.2 7.6 %all-to-all-start = ((bf16[16,512,512]{1,2,0:T(8,128)(2,1)}), bf16[16,512,512]{1,2,0:T(8,128)(2,1)}, u32[]{:S(2)}, u32[]{:S(2)}) async-start(bf16[16,512,512]{1,2,0:T(8,128)(2,1)} %stack.2), calls=%async_computation | async-start | bytes 16777216 | tf_op jit(solution)/shard_map/all_to_all | solution.py:25
  21.9 2.6 iota_compare_fusion
  24.5 9.4 %fusion.3 = f32[128,256,16]{1,2,0:T(8,128)} fusion(pred[128,128,256]{2,1,0:T(32,128)(4,1)S(1)} %iota_compare_fusion, f32[128,16]{0,1:T(8,128)S(1)} %copy-done), kind=kOutput, calls=%fused_computation.6 | convolution fusion | flops 805306368 | bytes 6299648 | tf_op jit(solution)/shard_map/jg,jis->gis/dot_general | solution.py:55
  33.9 208.0 %all-to-all-done = bf16[16,512,512]{1,2,0:T(8,128)(2,1)} async-done(((bf16[16,512,512]{1,2,0:T(8,128)(2,1)}), bf16[16,512,512]{1,2,0:T(8,128)(2,1)}, u32[]{:S(2)}, u32[]{:S(2)}) %all-to-all-start) | async-done | bytes 8388640 | tf_op jit(solution)/shard_map/all_to_all | solution.py:25
  241.9 5.2 %fusion = f32[512]{0:T(512)S(1)} fusion(bf16[16,512,512]{1,2,0:T(8,128)(2,1)} %all-to-all-done), kind=kLoop, calls=%fused_computation.2 | loop fusion | flops 12582400 | bytes 8390656 | tf_op jit(solution)/shard_map/reduce_sum | solution.py:28
  247.1 7.7 %fusion.2 = bf16[16,512,512]{1,2,0:T(8,128)(2,1)} fusion(bf16[16,512,512]{1,2,0:T(8,128)(2,1)} %all-to-all-done, f32[16,512]{1,0:T(8,128)S(1)} %mul.77, f32[512]{0:T(512)S(1)} %add_rsqrt_fusion), kind=kLoop, calls=%fused_computation.4 | loop fusion | flops 16777216 | bytes 16812032 | tf_op jit(solution)/shard_map/convert_element_type | solution.py:29
  254.8 12.9 %convolution_convert_fusion.1 = bf16[512,768]{1,0:T(8,128)(2,1)S(1)} fusion(bf16[512,8192]{0,1:T(8,128)(2,1)} %bitcast.52, bf16[8192,768]{0,1:T(8,128)(2,1)} %bitcast.55), kind=kOutput, calls=%fused_computation.17 | convolution fusion | flops 6442844160 | bytes 21757952 | tf_op jit(solution)/shard_map/dot_general | solution.py:32
  267.7 1.3 collective-permute-start
  269.4 1.0 collective-permute-done
  270.5 0.5 pad_maximum_fusion
  271.2 1.4 fusion.8
  272.7 4.4 %collective-permute-start.1 = (bf16[127,256]{0,1:T(8,128)(2,1)S(1)}, bf16[127,256]{0,1:T(8,128)(2,1)S(1)}, u32[]{:S(2)}, u32[]{:S(2)}) collective-permute-start(bf16[127,256]{0,1:T(8,128)(2,1)S(1)} %slice_bitcast_fusion.1), channel_id=1, source_target_pairs={{0,16},{16,32},{32,48},{48,64},{64,80},{80,96},{96,112},{112,128},... | collective-permute-start | bytes 195080 | tf_op jit(solution)/shard_map/ppermute | solution.py:14
  277.3 1.5 collective-permute-done.1
  279.4 1.0 concatenate.20
  280.3 1.1 copy.16
  281.4 1.0 concatenate.21
  282.4 1.2 copy.17
  283.6 5.2 %fusion.10 = f32[4,128,16,16]{1,3,0,2:T(8,128)S(1)} fusion(f32[128,256,16]{1,2,0:T(8,128)} %fusion.3, f32[4,128,16,16]{1,3,0,2:T(8,128)S(1)} %copy.17, f32[4,128,16,16]{1,3,0,2:T(8,128)S(1)} %copy.16), kind=kOutput, calls=%fused_computation.18 | convolution fusion | flops 402915328 | bytes 3670016 | tf_op jit(solution)/shard_map/gis,bsgc->bigc/dot_general | solution.py:58
  289.0 5.9 %convolution_convert_fusion = bf16[512,8192]{1,0:T(8,128)(2,1)} fusion(bf16[256,8192]{1,0:T(8,128)(2,1)S(1)} %copy-done.2, f32[32,8,4,128]{3,2,1,0:T(4,128)S(1)} %bitcast.54, f32[512,3,256]{0,2,1:T(8,128)S(1)} %fusion.8, f32[256]{0:T(256)S(1)} %copy-done.5, f32[639,256]{0,1:T(8,128)S(1)} %convert_element_type.57), kind=kOutput, calls=%fused_computation.8 | convolution fusion | flops 2152202240 | bytes 14156800 | tf_op jit(solution)/shard_map/dot_general | solution.py:61
  295.0 111.5 %reduce-scatter.2.cloned.1.call-done = bf16[512,512]{1,0:T(8,128)(2,1)} async-done(((bf16[512,8192]{1,0:T(8,128)(2,1)}), bf16[512,512]{1,0:T(8,128)(2,1)}) %reduce-scatter.2.cloned.1.call-update) | async-done | bytes 524304 | tf_op jit(solution)/shard_map/reduce_scatter | solution.py:63
  406.5 2.0 add_convert_fusion
  (36 shorter events, 1.7 us)
Async XLA Ops:
  6.5 18.0 %copy-start = (f32[128,16]{0,1:T(8,128)S(1)}, f32[128,16]{0,1:T(8,128)}, u32[]{:S(2)}) copy-start(f32[128,16]{0,1:T(8,128)} %param.11) | copy-start | bytes 24580
  6.5 248.3 %all-gather.2.cloned.1.call-start = ((), (), s32[]{:S(2)}) async-start(), calls=%async_computation.2 | async-start | bytes 13369344 | tf_op jit(solution)/shard_map/all_gather | solution.py:30
  14.2 7.7 %copy-start.4 = (f32[8192]{0:T(1024)S(1)}, f32[8192]{0:T(1024)}, u32[]{:S(2)}) copy-start(f32[8192]{0:T(1024)} %param.8) | copy-start | bytes 98308
  14.2 227.7 %all-to-all-start = ((bf16[16,512,512]{1,2,0:T(8,128)(2,1)}), bf16[16,512,512]{1,2,0:T(8,128)(2,1)}, u32[]{:S(2)}, u32[]{:S(2)}) async-start(bf16[16,512,512]{1,2,0:T(8,128)(2,1)} %stack.2), calls=%async_computation | async-start | bytes 16777216 | tf_op jit(solution)/shard_map/all_to_all | solution.py:25
  21.8 384.7 %reduce-scatter.2.cloned.1.call-start = ((), (), s32[]{:S(2)}) async-start(), calls=%async_computation.3 | async-start | bytes 8912896 | tf_op jit(solution)/shard_map/reduce_scatter | solution.py:63
  254.8 14.2 %copy-start.6 = (f32[3,3,256]{2,1,0:T(4,128)S(1)}, f32[3,3,256]{2,1,0:T(4,128)}, u32[]{:S(2)}) copy-start(f32[3,3,256]{2,1,0:T(4,128)} %param.10) | copy-start | bytes 27652
  267.7 2.6 collective-permute-start
  272.7 6.1 %collective-permute-start.1 = (bf16[127,256]{0,1:T(8,128)(2,1)S(1)}, bf16[127,256]{0,1:T(8,128)(2,1)S(1)}, u32[]{:S(2)}, u32[]{:S(2)}) collective-permute-start(bf16[127,256]{0,1:T(8,128)(2,1)S(1)} %slice_bitcast_fusion.1), channel_id=1, source_target_pairs={{0,16},{16,32},{32,48},{48,64},{64,80},{80,96},{96,112},{112,128},... | collective-permute-start | bytes 195080 | tf_op jit(solution)/shard_map/ppermute | solution.py:14
  280.3 8.7 %copy-start.5 = (f32[256]{0:T(256)S(1)}, f32[256]{0:T(256)}, u32[]{:S(2)}) copy-start(f32[256]{0:T(256)} %param.12) | copy-start | bytes 3076
  282.4 6.6 %copy-start.2 = (bf16[256,8192]{1,0:T(8,128)(2,1)S(1)}, bf16[256,8192]{1,0:T(8,128)(2,1)}, u32[]{:S(2)}) copy-start(bf16[256,8192]{1,0:T(8,128)(2,1)} %param.13) | copy-start | bytes 12582916
  295.0 113.5 %copy-start.1 = (f32[128,16]{0,1:T(8,128)S(1)}, f32[128,16]{0,1:T(8,128)}, u32[]{:S(2)}) copy-start(f32[128,16]{0,1:T(8,128)} %param.11) | copy-start | bytes 24580
  295.0 111.6 %copy-start.3 = (bf16[512,512]{1,0:T(8,128)(2,1)S(1)}, bf16[512,512]{1,0:T(8,128)(2,1)}, u32[]{:S(2)}) copy-start(bf16[512,512]{1,0:T(8,128)(2,1)} %param.7) | copy-start | bytes 1572868
Sparse Core Ops, SparseCore 0:
  9.2 210.2 all-gather.1
  295.1 111.3 reduce-scatter.1
